TPU v7x, 128 devices: a whole 4x4x4 slice. The times are simulated.
128 devices in a mesh: seq: 4 (over y_lo, core), blk: 32 (over x, y_hi, z).
Axes of the slice: x: 4, y: 4 (y_hi: 2, y_lo: 2; y = y_hi * 2 + y_lo), z: 4, core: 2. Of those that a mesh axis runs over, the one named last changes fastest.
Arguments:
- tokens: bfloat16 [32768, 8192], P(('seq', 'blk')), may hold values from -21 to 21
- query_weight: bfloat16 [8192, 1024], replicated, may hold values from -0.0625 to 0.0625
- key_weight: bfloat16 [8192, 128], replicated, may hold values from -0.0625 to 0.0625
- value_weight: bfloat16 [8192, 128], replicated, may hold values from -0.0625 to 0.0625
- doc_lengths: int32 [4, 4], replicated, may hold values from 1 to 4096, 8192 in all within a row
- slot_index: int32 [32768], P(('seq', 'blk')), may hold values from 0 to 32767, as said below
Outputs:
- attended: bfloat16 [32768, 1024], P(('seq', 'blk'))
Inputs may be any that keep to these rules, and one draw needn't show every extreme that they name: `slot_index`: each value appears exactly once. The 256 rows of one loader device put at most 3 rows into the 256 consecutive slots k * 256 to (k + 1) * 256 - 1 of any k, and exactly 3 into some of them.
All inputs are finite; a program needn't handle non-finite values.
Results may differ from a plain program's by a relative error of at most 0.0085.
The roundings to bfloat16 on the way count: a program that leaves them out, or rounds other values in their place, can miss the bound.
Values may be sent and summed in bfloat16 or wider, within the bound.
A program may use at most 128 MiB of HBM per device.

v0:
```python
import math
import jax
import jax.numpy as jnp
from jax import lax
from jax.sharding import PartitionSpec as P

HQ = 8
HS = 128


def rotate_pairs(values, positions):
    half_width = values.shape[-1] // 2
    frequency = 500000.0 ** (-(jnp.arange(half_width, dtype=jnp.float32) * 2.0 / values.shape[-1]))
    angles = positions.astype(jnp.float32)[:, None, None] * frequency[None, None, :]
    cosine = jnp.cos(angles)
    sine_values = jnp.sin(angles)
    leading = values[..., :half_width]
    trailing = values[..., half_width:]
    return jnp.concatenate(
        [leading * cosine - trailing * sine_values, trailing * cosine + leading * sine_values],
        axis=-1,
    )


def doc_positions(lengths_table, local_slot):
    doc_ends = jnp.cumsum(lengths_table, axis=-1)
    starts = doc_ends - lengths_table
    document = jnp.sum((local_slot[:, None] >= doc_ends).astype(jnp.int32), axis=1)
    picked = jnp.arange(lengths_table.shape[-1], dtype=jnp.int32)[None, :] == document[:, None]
    start_of = jnp.sum(jnp.where(picked, starts, 0), axis=1)
    return (document, local_slot - start_of)


def place_slot(local_slot, rows_dev):
    return (local_slot // rows_dev, local_slot % rows_dev)


def slot_of(device, row_index, rows_dev):
    return device * rows_dev + row_index


def project_rows(rows, query_weight, key_weight, value_weight):
    lead_shape = rows.shape[:-1]
    flat_rows = rows.reshape(-1, rows.shape[-1])
    results = []
    for weight in (query_weight, key_weight, value_weight):
        product = jnp.dot(flat_rows, weight, preferred_element_type=jnp.float32)
        results.append(product.reshape(lead_shape + (weight.shape[1],)))
    return (results[0], results[1], results[2])


def finish_rows(query_f, key_f, value_f, positions):
    row_count = query_f.shape[0]
    query_rows = (
        rotate_pairs(query_f.reshape(row_count, HQ, HS), positions)
        .reshape(row_count, HQ * HS)
        .astype(jnp.bfloat16)
    )
    key_rows = rotate_pairs(key_f[:, None, :], positions)[:, 0, :].astype(jnp.bfloat16)
    return (query_rows, key_rows, value_f.astype(jnp.bfloat16))


def arrange_rows(values, where_flat, rows_dev):
    width = values.shape[-1]
    empty = jnp.zeros((rows_dev, width), values.dtype)
    return empty.at[where_flat].set(values.reshape(-1, width), mode="drop")


def shards(tokens, query_weight, key_weight, value_weight, doc_lengths, slot_index):
    rows_dev = tokens.shape[0]
    device_count = lax.axis_size(("seq", "blk"))
    block_count = lax.axis_size("blk")
    group_rows = block_count * rows_dev
    capacity = rows_dev // device_count + 1
    seq_position = lax.axis_index("seq")
    block_position = lax.axis_index("blk")
    seq_count = doc_lengths.shape[0]
    group_of = slot_index // group_rows
    local_of = slot_index % group_rows
    target_block, target_row = place_slot(local_of, rows_dev)
    target = group_of * block_count + target_block
    same_target = target[:, None] == target[None, :]
    row_order = jnp.arange(rows_dev, dtype=jnp.int32)
    earlier = row_order[None, :] < row_order[:, None]
    rank = jnp.sum((same_target & earlier).astype(jnp.int32), axis=1)
    flat_index = target * capacity + rank
    where_send = (
        jnp.full((device_count * capacity,), rows_dev, jnp.int32).at[flat_index].set(target_row)
    )
    where_send = where_send.reshape(device_count, capacity)
    my_local = slot_of(block_position, row_order, rows_dev)
    group_pick = jnp.arange(seq_count, dtype=jnp.int32)[:, None] == seq_position
    my_lengths = jnp.sum(jnp.where(group_pick, doc_lengths, 0), axis=0)[None, :]
    my_doc, my_pos = doc_positions(my_lengths, my_local)
    outgoing = (
        jnp.zeros((device_count * capacity, tokens.shape[1]), jnp.bfloat16)
        .at[flat_index]
        .set(tokens)
    )
    outgoing = outgoing.reshape(device_count, capacity, tokens.shape[1])
    rows_in = lax.all_to_all(outgoing, ("seq", "blk"), split_axis=0, concat_axis=0, tiled=True)
    where_in = lax.all_to_all(where_send, ("seq", "blk"), split_axis=0, concat_axis=0, tiled=True)
    query_f, key_f, value_f = project_rows(rows_in, query_weight, key_weight, value_weight)
    query_f, key_f, value_f, where_recv = (query_f, key_f, value_f, where_in)
    where_flat = where_recv.reshape(-1)
    query_rows, key_rows, value_rows = finish_rows(
        arrange_rows(query_f, where_flat, rows_dev),
        arrange_rows(key_f, where_flat, rows_dev),
        arrange_rows(value_f, where_flat, rows_dev),
        my_pos,
    )
    query_three = query_rows.reshape(rows_dev, HQ, HS)
    score_scale = 1.0 / math.sqrt(HS)
    initial = (
        jnp.full((rows_dev, HQ), -1e30, jnp.float32),
        jnp.zeros((rows_dev, HQ), jnp.float32),
        jnp.zeros((rows_dev, HQ, HS), jnp.float32),
    )
    key_piece = lax.all_gather(key_rows, "blk", axis=0, tiled=True)
    value_piece = lax.all_gather(value_rows, "blk", axis=0, tiled=True)
    key_count = key_piece.shape[0]
    block_width = math.gcd(key_count, 512)
    gathered_rows = jnp.arange(key_count, dtype=jnp.int32)
    key_local = slot_of(gathered_rows // rows_dev, gathered_rows % rows_dev, rows_dev)
    key_doc, unused_pos = doc_positions(my_lengths, key_local)

    def one_block(block_number, running):
        offset = block_number * block_width
        key_block = lax.dynamic_slice_in_dim(key_piece, offset, block_width, 0)
        value_block = lax.dynamic_slice_in_dim(value_piece, offset, block_width, 0)
        local_block = lax.dynamic_slice_in_dim(key_local, offset, block_width, 0)
        doc_block = lax.dynamic_slice_in_dim(key_doc, offset, block_width, 0)
        allowed = (my_doc[:, None] == doc_block[None, :]) & (
            local_block[None, :] <= my_local[:, None]
        )

        def update(current):
            running_max, denominator, numerator = current
            scores = (
                jnp.einsum(
                    "qhd,kd->qhk", query_three, key_block, preferred_element_type=jnp.float32
                )
                * score_scale
            )
            allowed_three = allowed[:, None, :]
            scores = jnp.where(allowed_three, scores, -1e30)
            new_max = jnp.maximum(running_max, jnp.max(scores, axis=-1))
            weights = jnp.where(allowed_three, jnp.exp(scores - new_max[..., None]), 0.0)
            factor = jnp.exp(running_max - new_max)
            denominator = denominator * factor + jnp.sum(weights, axis=-1)
            numerator = numerator * factor[..., None] + jnp.einsum(
                "qhk,kd->qhd",
                weights.astype(jnp.bfloat16),
                value_block,
                preferred_element_type=jnp.float32,
            )
            return (new_max, denominator, numerator)

        def unchanged(current):
            return current

        return lax.cond(jnp.any(allowed), update, unchanged, running)

    final_max, denominator, numerator = lax.fori_loop(
        0, key_count // block_width, one_block, initial
    )
    attended_rows = (
        (numerator / denominator[..., None]).reshape(rows_dev, HQ * HS).astype(jnp.bfloat16)
    )
    is_filled = (where_flat < rows_dev).astype(jnp.bfloat16)
    returning = (
        jnp.take(attended_rows, jnp.minimum(where_flat, rows_dev - 1), axis=0) * is_filled[:, None]
    )
    returning = returning.reshape(device_count, capacity, HQ * HS)
    returned = lax.all_to_all(returning, ("seq", "blk"), split_axis=0, concat_axis=0, tiled=True)
    return jnp.take(returned.reshape(-1, HQ * HS), flat_index, axis=0)


def solution(mesh):
    in_specs = (P(("seq", "blk"), None), P(), P(), P(), P(), P(("seq", "blk")))
    out_specs = P(("seq", "blk"), None)
    return jax.shard_map(shards, mesh=mesh, in_specs=in_specs, out_specs=out_specs, check_vma=False)
```

profile of v0, /device:TPU:1, one launch (start us, length us, event | category | flops | bytes accessed | tf_op | source)
XLA Modules:
  0.0 446.0 jit_solution(17842980668918397970)
XLA Ops:
  6.5 0.8 and_select_fusion
  7.4 0.7 fusion.50
  8.3 1.4 scatter_custom_fusion
  9.7 0.8 all_to_all.12
  10.5 11.5 %all-to-all-start = ((s32[128,1,3]{2,1,0:T(1,128)}), s32[128,1,3]{2,1,0:T(1,128)S(1)}, u32[]{:S(2)}, u32[]{:S(2)}) async-start(s32[128,1,3]{2,1,0:T(1,128)} %bitcast.3), calls=%async_computation | async-start | bytes 131072 | tf_op jit(solution)/shard_map/all_to_all | solution.py:102
  22.0 11.3 %scatter_custom_fusion.1 = bf16[384,8192]{1,0:T(8,128)(2,1)} fusion(s32[256]{0:T(256)S(1)} %get-tuple-element.406, bf16[256,8192]{1,0:T(8,128)(2,1)} %param.10, bf16[]{:T(256)} %constant.190.clone.1), kind=kCustom, calls=%fused_computation.30 | custom fusion | bytes 6291968 | tf_op jit(solution)/shard_map/scatter | solution.py:98
  33.3 12.8 %reshape.294 = bf16[128,3,8192]{2,1,0:T(4,128)(2,1)} reshape(bf16[384,8192]{1,0:T(8,128)(2,1)} %scatter_custom_fusion.1) | data formatting | bytes 12582912 | tf_op jit(solution)/shard_map/reshape | solution.py:100
  46.1 10.2 %all-to-all-start.1 = ((bf16[128,3,8192]{2,1,0:T(4,128)(2,1)}), bf16[128,3,8192]{2,1,0:T(4,128)(2,1)}, u32[]{:S(2)}, u32[]{:S(2)}) async-start(bf16[128,3,8192]{2,1,0:T(4,128)(2,1)} %reshape.294), calls=%async_computation.1 | async-start | bytes 16777216 | tf_op jit(solution)/shard_map/all_to_all | solution.py:101
  57.6 0.8 broadcast_minimum_fusion
  58.7 105.3 %all-to-all-done.1 = bf16[128,3,8192]{2,1,0:T(4,128)(2,1)} async-done(((bf16[128,3,8192]{2,1,0:T(4,128)(2,1)}), bf16[128,3,8192]{2,1,0:T(4,128)(2,1)}, u32[]{:S(2)}, u32[]{:S(2)}) %all-to-all-start.1) | async-done | bytes 6291488 | tf_op jit(solution)/shard_map/all_to_all | solution.py:101
  164.0 13.8 %reshape.295 = bf16[384,8192]{1,0:T(8,128)(2,1)} reshape(bf16[128,3,8192]{2,1,0:T(4,128)(2,1)} %all-to-all-done.1) | data formatting | bytes 12582912 | tf_op jit(solution)/shard_map/reshape | solution.py:44
  177.8 4.6 %fusion.54 = f32[384,128]{1,0:T(8,128)S(1)} fusion(bf16[384,8192]{1,0:T(8,128)(2,1)} %reshape.295, bf16[8192,128]{1,0:T(8,128)(2,1)S(1)} %copy-done), kind=kOutput, calls=%fused_computation.115 | convolution fusion | flops 805306368 | bytes 8585216 | tf_op jit(solution)/shard_map/dot_general | solution.py:47
  182.3 1.5 scatter_custom_fusion.2
  184.9 5.2 %fusion.56 = f32[384,128]{1,0:T(8,128)S(1)} fusion(bf16[384,8192]{1,0:T(8,128)(2,1)} %reshape.295, bf16[8192,128]{1,0:T(8,128)(2,1)} %param.13), kind=kOutput, calls=%fused_computation.117 | convolution fusion | flops 805306368 | bytes 8585216 | tf_op jit(solution)/shard_map/dot_general | solution.py:47
  190.1 1.5 scatter_custom_fusion.4
  193.0 13.1 %fusion.55 = f32[384,1024]{1,0:T(8,128)} fusion(bf16[384,8192]{1,0:T(8,128)(2,1)} %reshape.295, bf16[8192,1024]{1,0:T(8,128)(2,1)} %param.11), kind=kOutput, calls=%fused_computation.116 | convolution fusion | flops 6442450944 | bytes 24641536 | tf_op jit(solution)/shard_map/dot_general | solution.py:47
  206.1 3.2 scatter_custom_fusion.3
  210.1 47.2 %all-gather.6.cloned.1.call-done = bf16[8192,1,128]{0,2,1:T(8,128)(2,1)} async-done(((bf16[256,1,128]{0,2,1:T(8,128)(2,1)}), bf16[8192,1,128]{0,2,1:T(8,128)(2,1)}) %all-gather.6.cloned.1.call-update) | async-done | bytes 2097168 | tf_op jit(solution)/shard_map/all_gather | solution.py:119
  257.3 4.1 copy.50
  261.4 69.5 %all-gather.4.cloned.1.call-done = bf16[8192,128]{1,0:T(8,128)(2,1)} async-done(((bf16[256,128]{1,0:T(8,128)(2,1)}), bf16[8192,128]{1,0:T(8,128)(2,1)}) %all-gather.4.cloned.1.call-update) | async-done | bytes 2097168 | tf_op jit(solution)/shard_map/all_gather | solution.py:120
  331.0 32.0 %while.18 = (s32[]{:T(128)}, f32[256,8]{0,1:T(8,128)S(1)}, f32[256,8]{0,1:T(8,128)S(1)}, f32[256,8,128]{2,0,1:T(8,128)S(1)}, s32[256]{0:T(256)S(1)}, /*index=5*/...) while((s32[]{:T(128)}, f32[256,8]{0,1:T(8,128)S(1)}, ...), condition=%wide.region_17.18_spmd.clone, body=%wide.region_11.17_spmd.clone.sunk | while | flops 551555328 | bytes 16138565 | solution.py:164
  331.1 0.8 fusion.66
  332.6 5.3 %conditional.3 = ((f32[256,8]{0,1:T(8,128)S(1)}, f32[256,8]{0,1:T(8,128)S(1)}, f32[256,8,128]{2,0,1:T(8,128)S(1)})) conditional(s32[]{:T(128)} %convert_element_type.80, (f32[256,8]{0,1:T(8,128)S(1)}, f32[256,8]{0,1:T(8,128)S(1)}, f32[256,8,128]{2,0,1:T(8,128)S(1)}) %tuple.65, (pred[256,512]{0,1:T(8,128)(4,1)S(1)}, bf16[8192,128]{1,0:T(8,128)(2,1)}, ...), branch_computations={%region_13.13_spmd, %region_14.16_spmd} | conditional | flops 551030784 | bytes 15991840 | solution.py:162
  332.6 1.7 fusion.2
  334.3 1.0 fusion.4
  335.4 2.5 fusion.8
  338.1 0.8 fusion.66
  339.8 0.8 fusion.66
  341.4 0.8 fusion.66
  343.1 0.8 fusion.66
  344.8 0.8 fusion.66
  346.4 0.8 fusion.66
  348.1 0.8 fusion.66
  349.8 0.8 fusion.66
  351.4 0.8 fusion.66
  353.1 0.8 fusion.66
  354.8 0.8 fusion.66
  356.5 0.8 fusion.66
  358.1 0.8 fusion.66
  359.8 0.8 fusion.66
  361.5 0.8 fusion.66
  363.3 2.1 gather_fusion
  365.9 1.7 select_multiply_fusion
  367.7 48.5 %all-to-all-start.2 = ((bf16[128,3,1024]{2,1,0:T(4,128)(2,1)}), bf16[128,3,1024]{2,1,0:T(4,128)(2,1)}, u32[]{:S(2)}, u32[]{:S(2)}) async-start(bf16[128,3,1024]{2,1,0:T(4,128)(2,1)} %select_multiply_fusion), calls=%async_computation.2 | async-start | bytes 2097152 | tf_op jit(solution)/shard_map/all_to_all | solution.py:175
  416.1 18.5 %all-to-all-done.2 = bf16[128,3,1024]{2,1,0:T(4,128)(2,1)} async-done(((bf16[128,3,1024]{2,1,0:T(4,128)(2,1)}), bf16[128,3,1024]{2,1,0:T(4,128)(2,1)}, u32[]{:S(2)}, u32[]{:S(2)}) %all-to-all-start.2) | async-done | bytes 786464 | tf_op jit(solution)/shard_map/all_to_all | solution.py:175
  434.7 2.4 reshape.297
  437.1 1.2 gather_fusion.1
  438.3 0.9 broadcast_select_fusion
  (113 shorter events, 8.5 us)
Async XLA Ops:
  6.5 171.2 %copy-start = (bf16[8192,128]{1,0:T(8,128)(2,1)S(1)}, bf16[8192,128]{1,0:T(8,128)(2,1)}, u32[]{:S(2)}) copy-start(bf16[8192,128]{1,0:T(8,128)(2,1)} %param.12) | copy-start | bytes 6291460
  10.5 35.6 %all-to-all-start = ((s32[128,1,3]{2,1,0:T(1,128)}), s32[128,1,3]{2,1,0:T(1,128)S(1)}, u32[]{:S(2)}, u32[]{:S(2)}) async-start(s32[128,1,3]{2,1,0:T(1,128)} %bitcast.3), calls=%async_computation | async-start | bytes 131072 | tf_op jit(solution)/shard_map/all_to_all | solution.py:102
  46.1 10.5 %copy-start.2 = (s32[4,4]{1,0:T(4,128)S(1)}, s32[4,4]{1,0:T(4,128)}, u32[]{:S(2)}) copy-start(s32[4,4]{1,0:T(4,128)} %param.14) | copy-start | bytes 196
  46.1 117.9 %all-to-all-start.1 = ((bf16[128,3,8192]{2,1,0:T(4,128)(2,1)}), bf16[128,3,8192]{2,1,0:T(4,128)(2,1)}, u32[]{:S(2)}, u32[]{:S(2)}) async-start(bf16[128,3,8192]{2,1,0:T(4,128)(2,1)} %reshape.294), calls=%async_computation.1 | async-start | bytes 16777216 | tf_op jit(solution)/shard_map/all_to_all | solution.py:101
  56.3 201.0 %all-gather.6.cloned.1.call-start = ((), (), s32[]{:S(2)}) async-start(), calls=%async_computation.4 | async-start | bytes 2162688 | tf_op jit(solution)/shard_map/all_gather | solution.py:119
  184.9 146.0 %all-gather.4.cloned.1.call-start = ((), (), s32[]{:S(2)}) async-start(), calls=%async_computation.3 | async-start | bytes 2162688 | tf_op jit(solution)/shard_map/all_gather | solution.py:120
  367.7 67.0 %all-to-all-start.2 = ((bf16[128,3,1024]{2,1,0:T(4,128)(2,1)}), bf16[128,3,1024]{2,1,0:T(4,128)(2,1)}, u32[]{:S(2)}, u32[]{:S(2)}) async-start(bf16[128,3,1024]{2,1,0:T(4,128)(2,1)} %select_multiply_fusion), calls=%async_computation.2 | async-start | bytes 2097152 | tf_op jit(solution)/shard_map/all_to_all | solution.py:175
  416.1 23.0 %copy-start.1 = (bf16[8192,128]{1,0:T(8,128)(2,1)S(1)}, bf16[8192,128]{1,0:T(8,128)(2,1)}, u32[]{:S(2)}) copy-start(bf16[8192,128]{1,0:T(8,128)(2,1)} %param.12) | copy-start | bytes 6291460
Sparse Core Ops, SparseCore 0:
  185.0 72.2 all-gather.5
  260.4 70.3 all-gather.3
where the time goes:
time: 448 us; the launch traced here: 446 us
  waiting for transfers between devices  241 us (54%)
  starting transfers between devices  70.4 us (16%)
  local copies, waits for them, and re-layouts  60.6 us (14%)
  matrix products  27.1 us (6%)
  other arithmetic  23 us (5%)
  between operations  13.7 us (3%)
  loops' own time  10.7 us (2%)
    all_to_all x1, waiting for transfers between devices, shards(): lax.all_to_all(outgoing, ('seq', 'blk'), split_axis=0, concat_axis=0, til...  105 us
    all_gather x1, waiting for transfers between devices, shards(): value_piece = lax.all_gather(value_rows, 'blk', axis=0, tiled=True)  69.5 us
    all_to_all x1, starting transfers between devices, shards(): lax.all_to_all(returning, ('seq', 'blk'), split_axis=0, concat_axis=0, ti...  48.5 us
    all_gather x1, waiting for transfers between devices, shards(): key_piece = lax.all_gather(key_rows, 'blk', axis=0, tiled=True)  47.2 us
    dot_general x3, matrix products, project_rows(): product = jnp.dot(flat_rows, weight, preferred_element_type=jnp.float32)  22.9 us
    all_to_all x1, waiting for transfers between devices, shards(): lax.all_to_all(returning, ('seq', 'blk'), split_axis=0, concat_axis=0, ti...  18.5 us
    reshape x1, local copies, waits for them, and re-layouts, project_rows(): flat_rows = rows.reshape(-1, rows.shape[-1])  13.8 us
    reduce_or x16, other arithmetic, one_block(): return lax.cond(jnp.any(allowed), update, unchanged, running)  13.6 us
  transfers between devices with their start and end apart: 5, of which 4 were waited for; matrix products, arithmetic and copies ran while one was open for 12% of the time, Pallas kernels for 0%

commit v1 on v0

--- a/solution.py
+++ b/solution.py
@@ -116,7 +116,10 @@
         jnp.zeros((rows_dev, HQ), jnp.float32),
         jnp.zeros((rows_dev, HQ, HS), jnp.float32),
     )
-    key_piece = lax.all_gather(key_rows, "blk", axis=0, tiled=True)
+    count = lax.axis_size("blk")
+    blocks = jnp.stack([key_rows for _ in range(count)])
+    blocks = lax.all_to_all(blocks, "blk", split_axis=0, concat_axis=0)
+    key_piece = jnp.concatenate(blocks, axis=0)
     value_piece = lax.all_gather(value_rows, "blk", axis=0, tiled=True)
     key_count = key_piece.shape[0]
     block_width = math.gcd(key_count, 512)

time: 448 us -> 395 us (0.88)
  waiting for transfers between devices: 241 us -> 180 us
  starting transfers between devices: 70.4 us -> 80.8 us
    all_gather x1 -> x0, waiting for transfers between devices: 47.2 us -> none  [shards(): key_piece = lax.all_gather(key_rows, 'blk', axis=0, tiled=True)]
    all_gather x1, waiting for transfers between devices: 69.5 us -> 47.8 us  [shards(): value_piece = lax.all_gather(value_rows, 'blk', axis=0, tiled=True)]
    all_to_all x0 -> x1, starting transfers between devices: none -> 10.4 us  [shards(): blocks = lax.all_to_all(blocks, 'blk', split_axis=0, concat_axis=0)]
    all_to_all x0 -> x1, waiting for transfers between devices: none -> 8.52 us  [shards(): blocks = lax.all_to_all(blocks, 'blk', split_axis=0, concat_axis=0)]
  transfers between devices with their start and end apart: 5 -> 5, of which waited for: 4 -> 4; matrix products, arithmetic and copies ran while one was open for 12% -> 13% of each run, Pallas kernels for 0% -> 0%
where the time goes in v1:
time: 395 us; the launch traced here: 393 us
  waiting for transfers between devices  180 us (46%)
  starting transfers between devices  80.8 us (20%)
  local copies, waits for them, and re-layouts  58.4 us (15%)
  matrix products  27.1 us (7%)
  other arithmetic  22.4 us (6%)
  between operations  13.7 us (3%)
  loops' own time  10.7 us (3%)
    all_to_all x1, waiting for transfers between devices, shards(): lax.all_to_all(outgoing, ('seq', 'blk'), split_axis=0, concat_axis=0, til...  105 us
    all_to_all x1, starting transfers between devices, shards(): lax.all_to_all(returning, ('seq', 'blk'), split_axis=0, concat_axis=0, ti...  48.5 us
    all_gather x1, waiting for transfers between devices, shards(): value_piece = lax.all_gather(value_rows, 'blk', axis=0, tiled=True)  47.8 us
    dot_general x3, matrix products, project_rows(): product = jnp.dot(flat_rows, weight, preferred_element_type=jnp.float32)  22.9 us
    all_to_all x1, waiting for transfers between devices, shards(): lax.all_to_all(returning, ('seq', 'blk'), split_axis=0, concat_axis=0, ti...  18.5 us
    reshape x1, local copies, waits for them, and re-layouts, project_rows(): flat_rows = rows.reshape(-1, rows.shape[-1])  13.8 us
    reduce_or x16, other arithmetic, one_block(): return lax.cond(jnp.any(allowed), update, unchanged, running)  13.6 us
    reshape x1, local copies, waits for them, and re-layouts, shards(): outgoing = outgoing.reshape(device_count, capacity, tokens.shape[1])  12.8 us
  transfers between devices with their start and end apart: 5, of which 4 were waited for; matrix products, arithmetic and copies ran while one was open for 13% of the time, Pallas kernels for 0%

profile of v1, /device:TPU:1, one launch (start us, length us, event | category | flops | bytes accessed | tf_op | source)
XLA Modules:
  0.0 393.2 jit_solution(1256144873318356759)
XLA Ops:
  6.5 0.8 and_select_fusion
  8.3 1.4 scatter_custom_fusion
  9.7 0.8 all_to_all.15
  10.5 11.5 %all-to-all-start = ((s32[128,1,3]{2,1,0:T(1,128)}), s32[128,1,3]{2,1,0:T(1,128)S(1)}, u32[]{:S(2)}, u32[]{:S(2)}) async-start(s32[128,1,3]{2,1,0:T(1,128)} %bitcast.3), calls=%async_computation | async-start | bytes 131072 | tf_op jit(solution)/shard_map/all_to_all | solution.py:102
  22.0 11.3 %scatter_custom_fusion.1 = bf16[384,8192]{1,0:T(8,128)(2,1)} fusion(s32[256]{0:T(256)S(1)} %get-tuple-element.406, bf16[256,8192]{1,0:T(8,128)(2,1)} %param.10, bf16[]{:T(256)} %constant.190.clone.1), kind=kCustom, calls=%fused_computation.30 | custom fusion | bytes 6291968 | tf_op jit(solution)/shard_map/scatter | solution.py:98
  33.3 12.8 %reshape.300 = bf16[128,3,8192]{2,1,0:T(4,128)(2,1)} reshape(bf16[384,8192]{1,0:T(8,128)(2,1)} %scatter_custom_fusion.1) | data formatting | bytes 12582912 | tf_op jit(solution)/shard_map/reshape | solution.py:100
  46.1 10.2 %all-to-all-start.1 = ((bf16[128,3,8192]{2,1,0:T(4,128)(2,1)}), bf16[128,3,8192]{2,1,0:T(4,128)(2,1)}, u32[]{:S(2)}, u32[]{:S(2)}) async-start(bf16[128,3,8192]{2,1,0:T(4,128)(2,1)} %reshape.300), calls=%async_computation.1 | async-start | bytes 16777216 | tf_op jit(solution)/shard_map/all_to_all | solution.py:101
  57.6 0.8 broadcast_minimum_fusion
  58.7 105.3 %all-to-all-done.1 = bf16[128,3,8192]{2,1,0:T(4,128)(2,1)} async-done(((bf16[128,3,8192]{2,1,0:T(4,128)(2,1)}), bf16[128,3,8192]{2,1,0:T(4,128)(2,1)}, u32[]{:S(2)}, u32[]{:S(2)}) %all-to-all-start.1) | async-done | bytes 6291488 | tf_op jit(solution)/shard_map/all_to_all | solution.py:101
  164.0 13.8 %reshape.301 = bf16[384,8192]{1,0:T(8,128)(2,1)} reshape(bf16[128,3,8192]{2,1,0:T(4,128)(2,1)} %all-to-all-done.1) | data formatting | bytes 12582912 | tf_op jit(solution)/shard_map/reshape | solution.py:44
  177.8 4.6 %fusion.56 = f32[384,128]{1,0:T(8,128)S(1)} fusion(bf16[384,8192]{1,0:T(8,128)(2,1)} %reshape.301, bf16[8192,128]{1,0:T(8,128)(2,1)S(1)} %copy-done), kind=kOutput, calls=%fused_computation.117 | convolution fusion | flops 805306368 | bytes 8585216 | tf_op jit(solution)/shard_map/dot_general | solution.py:47
  182.3 1.5 scatter_custom_fusion.4
  185.2 5.2 %fusion.54 = f32[384,128]{1,0:T(8,128)S(1)} fusion(bf16[384,8192]{1,0:T(8,128)(2,1)} %reshape.301, bf16[8192,128]{1,0:T(8,128)(2,1)} %param.12), kind=kOutput, calls=%fused_computation.115 | convolution fusion | flops 805306368 | bytes 8585216 | tf_op jit(solution)/shard_map/dot_general | solution.py:47
  190.4 1.5 scatter_custom_fusion.2
  192.5 1.8 stack.2
  194.3 10.4 %all-to-all-start.2 = ((bf16[32,256,128]{2,1,0:T(8,128)(2,1)}), bf16[32,256,128]{2,1,0:T(8,128)(2,1)}, u32[]{:S(2)}, u32[]{:S(2)}) async-start(bf16[32,256,128]{2,1,0:T(8,128)(2,1)} %stack.2), calls=%async_computation.2 | async-start | bytes 4194304 | tf_op jit(solution)/shard_map/all_to_all | solution.py:121
  204.7 13.1 %fusion.55 = f32[384,1024]{1,0:T(8,128)} fusion(bf16[384,8192]{1,0:T(8,128)(2,1)} %reshape.301, bf16[8192,1024]{1,0:T(8,128)(2,1)} %param.11), kind=kOutput, calls=%fused_computation.116 | convolution fusion | flops 6442450944 | bytes 24641536 | tf_op jit(solution)/shard_map/dot_general | solution.py:47
  217.8 3.2 scatter_custom_fusion.3
  221.8 8.5 %all-to-all-done.2 = bf16[32,256,128]{2,1,0:T(8,128)(2,1)} async-done(((bf16[32,256,128]{2,1,0:T(8,128)(2,1)}), bf16[32,256,128]{2,1,0:T(8,128)(2,1)}, u32[]{:S(2)}, u32[]{:S(2)}) %all-to-all-start.2) | async-done | bytes 2097184 | tf_op jit(solution)/shard_map/all_to_all | solution.py:121
  230.3 47.8 %all-gather.2.cloned.1.call-done = bf16[8192,128]{1,0:T(8,128)(2,1)} async-done(((bf16[256,128]{1,0:T(8,128)(2,1)}), bf16[8192,128]{1,0:T(8,128)(2,1)}) %all-gather.2.cloned.1.call-update) | async-done | bytes 2097168 | tf_op jit(solution)/shard_map/all_gather | solution.py:123
  278.2 32.0 %while.18 = (s32[]{:T(128)}, f32[256,8]{0,1:T(8,128)S(1)}, f32[256,8]{0,1:T(8,128)S(1)}, f32[256,8,128]{2,0,1:T(8,128)S(1)}, s32[256]{0:T(256)S(1)}, /*index=5*/...) while((s32[]{:T(128)}, f32[256,8]{0,1:T(8,128)S(1)}, ...), condition=%wide.region_17.18_spmd.clone, body=%wide.region_11.17_spmd.clone.sunk | while | flops 551555328 | bytes 16138565 | solution.py:167
  278.4 0.8 fusion.66
  279.9 5.3 %conditional.3 = ((f32[256,8]{0,1:T(8,128)S(1)}, f32[256,8]{0,1:T(8,128)S(1)}, f32[256,8,128]{2,0,1:T(8,128)S(1)})) conditional(s32[]{:T(128)} %convert_element_type.82, (f32[256,8]{0,1:T(8,128)S(1)}, f32[256,8]{0,1:T(8,128)S(1)}, f32[256,8,128]{2,0,1:T(8,128)S(1)}) %tuple.65, (pred[256,512]{0,1:T(8,128)(4,1)S(1)}, bf16[8192,128]{1,0:T(8,128)(2,1)}, ...), branch_computations={%region_13.13_spmd, %region_14.16_spmd} | conditional | flops 551030784 | bytes 15991840 | solution.py:165
  279.9 1.7 fusion.2
  281.6 1.0 fusion.4
  282.6 2.5 fusion.8
  285.3 0.8 fusion.66
  287.0 0.8 fusion.66
  288.7 0.8 fusion.66
  290.3 0.8 fusion.66
  292.0 0.8 fusion.66
  293.7 0.8 fusion.66
  295.3 0.8 fusion.66
  297.0 0.8 fusion.66
  298.7 0.8 fusion.66
  300.4 0.8 fusion.66
  302.0 0.8 fusion.66
  303.7 0.8 fusion.66
  305.4 0.8 fusion.66
  307.0 0.8 fusion.66
  308.7 0.8 fusion.66
  310.5 2.1 gather_fusion
  313.1 1.7 select_multiply_fusion
  314.9 48.5 %all-to-all-start.3 = ((bf16[128,3,1024]{2,1,0:T(4,128)(2,1)}), bf16[128,3,1024]{2,1,0:T(4,128)(2,1)}, u32[]{:S(2)}, u32[]{:S(2)}) async-start(bf16[128,3,1024]{2,1,0:T(4,128)(2,1)} %select_multiply_fusion), calls=%async_computation.3 | async-start | bytes 2097152 | tf_op jit(solution)/shard_map/all_to_all | solution.py:178
  363.4 18.5 %all-to-all-done.3 = bf16[128,3,1024]{2,1,0:T(4,128)(2,1)} async-done(((bf16[128,3,1024]{2,1,0:T(4,128)(2,1)}), bf16[128,3,1024]{2,1,0:T(4,128)(2,1)}, u32[]{:S(2)}, u32[]{:S(2)}) %all-to-all-start.3) | async-done | bytes 786464 | tf_op jit(solution)/shard_map/all_to_all | solution.py:178
  381.9 2.4 reshape.304
  384.3 1.2 gather_fusion.1
  385.5 0.9 broadcast_select_fusion
  (113 shorter events, 8.6 us)
Async XLA Ops:
  6.5 171.2 %copy-start = (bf16[8192,128]{1,0:T(8,128)(2,1)S(1)}, bf16[8192,128]{1,0:T(8,128)(2,1)}, u32[]{:S(2)}) copy-start(bf16[8192,128]{1,0:T(8,128)(2,1)} %param.13) | copy-start | bytes 6291460
  10.5 35.6 %all-to-all-start = ((s32[128,1,3]{2,1,0:T(1,128)}), s32[128,1,3]{2,1,0:T(1,128)S(1)}, u32[]{:S(2)}, u32[]{:S(2)}) async-start(s32[128,1,3]{2,1,0:T(1,128)} %bitcast.3), calls=%async_computation | async-start | bytes 131072 | tf_op jit(solution)/shard_map/all_to_all | solution.py:102
  46.1 10.5 %copy-start.2 = (s32[4,4]{1,0:T(4,128)S(1)}, s32[4,4]{1,0:T(4,128)}, u32[]{:S(2)}) copy-start(s32[4,4]{1,0:T(4,128)} %param.14) | copy-start | bytes 196
  46.1 117.9 %all-to-all-start.1 = ((bf16[128,3,8192]{2,1,0:T(4,128)(2,1)}), bf16[128,3,8192]{2,1,0:T(4,128)(2,1)}, u32[]{:S(2)}, u32[]{:S(2)}) async-start(bf16[128,3,8192]{2,1,0:T(4,128)(2,1)} %reshape.300), calls=%async_computation.1 | async-start | bytes 16777216 | tf_op jit(solution)/shard_map/all_to_all | solution.py:101
  56.3 221.8 %all-gather.2.cloned.1.call-start = ((), (), s32[]{:S(2)}) async-start(), calls=%async_computation.4 | async-start | bytes 2162688 | tf_op jit(solution)/shard_map/all_gather | solution.py:123
  194.3 36.0 %all-to-all-start.2 = ((bf16[32,256,128]{2,1,0:T(8,128)(2,1)}), bf16[32,256,128]{2,1,0:T(8,128)(2,1)}, u32[]{:S(2)}, u32[]{:S(2)}) async-start(bf16[32,256,128]{2,1,0:T(8,128)(2,1)} %stack.2), calls=%async_computation.2 | async-start | bytes 4194304 | tf_op jit(solution)/shard_map/all_to_all | solution.py:121
  314.9 67.0 %all-to-all-start.3 = ((bf16[128,3,1024]{2,1,0:T(4,128)(2,1)}), bf16[128,3,1024]{2,1,0:T(4,128)(2,1)}, u32[]{:S(2)}, u32[]{:S(2)}) async-start(bf16[128,3,1024]{2,1,0:T(4,128)(2,1)} %select_multiply_fusion), calls=%async_computation.3 | async-start | bytes 2097152 | tf_op jit(solution)/shard_map/all_to_all | solution.py:178
  363.3 23.0 %copy-start.1 = (bf16[8192,128]{1,0:T(8,128)(2,1)S(1)}, bf16[8192,128]{1,0:T(8,128)(2,1)}, u32[]{:S(2)}) copy-start(bf16[8192,128]{1,0:T(8,128)(2,1)} %param.13) | copy-start | bytes 6291460
Sparse Core Ops, SparseCore 0:
  184.6 93.4 all-gather.1
